TPU v7x, 32 devices: a whole 2x2x4 slice. The times are simulated.
32 devices in a mesh: dp: 32 (over z, y, x, core), mp: 1.
Axes of the slice: x: 2, y: 2, z: 4, core: 2. Of those that a mesh axis runs over, the one named last changes fastest.
Arguments:
- candidates: bfloat16 [32768, 256], P('dp', 'mp'), may hold values from 0 to 1, as said below
- first_weight: bfloat16 [256, 4096], P(None, 'mp'), may hold values from -48 to 48
- first_bias: bfloat16 [1, 4096], P(None, 'mp'), may hold values from -3 to 3
- second_weight: bfloat16 [4096, 4096], P(None, 'mp'), may hold values from -0.09375 to 0.09375
- second_bias: float32 [4096], P('mp'), may hold values from -3 to 3
- head_weight: float32 [4096], P('mp'), may hold values from -0.09375 to 0.09375
- owners: int32 [1024, 1], P('dp'), may hold values from 0 to 31; in each aligned block of 32 rows (0 to 31, 32 to 63, ...) at most 2 rows name the same one
Outputs:
- collected: bfloat16 [2048, 32, 256], P('dp', None, 'mp')
- collected_scores: bfloat16 [2048, 32], P('dp')
Inputs may be any that keep to these rules, and one draw needn't show every extreme that they name: `candidates`: each row is nonnegative and sums to one. `owners`: among the 32 blocks of one index of dp no collector is named more than 2 times, a bound that some block reaches.
All inputs are finite; a program needn't handle non-finite values.
Results may differ from a plain program's by a relative error of at most 0.0033.
Values may be sent and summed in bfloat16 or wider, within the bound.
No kernel may reach another device: no remote copies, remote signals or barrier semaphores. Data moves between devices by JAX's collectives and lax.ppermute only.
A program may use at most 128 MiB of HBM per device.

v0:
```python
import jax
import jax.numpy as jnp
from jax import lax
from jax.sharding import PartitionSpec as P

BROWS = 32
PAIR = 2


def local(candidates, first_weight, first_bias, second_weight, second_bias, head_weight, owners):
    slice_width = candidates.shape[1]
    full_rows = lax.all_gather(candidates, "mp", axis=1, tiled=True)
    first_local = jnp.dot(
        full_rows, first_weight, preferred_element_type=jnp.float32
    ) + first_bias.astype(jnp.float32)
    hidden = jnp.maximum(first_local, 0.0).astype(jnp.bfloat16)
    second = jnp.dot(
        lax.all_gather(hidden, "mp", axis=1, tiled=True),
        second_weight,
        preferred_element_type=jnp.float32,
    )
    hidden_two = jnp.maximum(second + second_bias, 0.0)
    partial_score = jnp.dot(hidden_two, head_weight, precision=lax.Precision.HIGHEST)
    scores = lax.psum(partial_score, "mp")
    block_count = owners.shape[0]
    collectors = lax.axis_size("dp")
    owner_list = owners[:, 0]
    same_owner = owner_list[:, None] == owner_list[None, :]
    before = lax.broadcasted_iota(jnp.int32, (block_count, block_count), 0) < lax.broadcasted_iota(
        jnp.int32, (block_count, block_count), 1
    )
    earlier_count = jnp.sum(jnp.where(same_owner & before, 1, 0), axis=0).astype(jnp.int32)
    target = owner_list * PAIR + earlier_count
    slot_index = jnp.arange(collectors * PAIR, dtype=jnp.int32)
    chooser = slot_index[:, None] == target[None, :]
    block_rows = candidates.reshape(block_count, BROWS * slice_width)
    outgoing = jnp.dot(chooser.astype(jnp.bfloat16), block_rows, preferred_element_type=jnp.float32)
    outgoing = outgoing.astype(jnp.bfloat16).reshape(collectors, PAIR, BROWS, slice_width)
    score_blocks = scores.reshape(block_count, BROWS)
    outgoing_scores = jnp.dot(
        chooser.astype(jnp.float32), score_blocks, precision=lax.Precision.HIGHEST
    )
    outgoing_scores = outgoing_scores.astype(jnp.bfloat16).reshape(collectors, PAIR, BROWS)
    arrived, arrived_scores = (
        lax.all_to_all(outgoing, "dp", split_axis=0, concat_axis=0, tiled=True),
        lax.all_to_all(outgoing_scores, "dp", split_axis=0, concat_axis=0, tiled=True),
    )
    collected = arrived.reshape(collectors * PAIR, BROWS, slice_width)
    collected_scores = arrived_scores.reshape(collectors * PAIR, BROWS)
    return (collected, collected_scores)


def solution(mesh):
    placed = (
        P("dp", "mp"),
        P(None, "mp"),
        P(None, "mp"),
        P(None, "mp"),
        P("mp"),
        P("mp"),
        P("dp", None),
    )
    return jax.shard_map(
        local,
        mesh=mesh,
        in_specs=placed,
        out_specs=(P("dp", None, "mp"), P("dp", None)),
        check_vma=False,
    )
```

profile of v0, /device:TPU:0, one launch (start us, length us, event | category | flops | bytes accessed | tf_op | source)
XLA Modules:
  0.0 111.9 jit_solution(7865769196238391831)
XLA Ops:
  0.6 0.0 copy-start
  0.6 0.9 select_reduce_fusion
  1.6 0.7 multiply_add_fusion
  2.2 0.7 add.36
  3.0 0.0 copy-done
  3.0 6.6 %maximum_convert_fusion.clone.4 = bf16[1024,4096]{1,0:T(8,128)(2,1)} fusion(bf16[1024,256]{1,0:T(8,128)(2,1)} %param.7, bf16[256,4096]{1,0:T(8,128)(2,1)S(1)} %copy-done, f32[4096]{0:T(1024)S(1)} %bitcast.30), kind=kOutput, calls=%fused_computation.3.clone.clone.clone.1 | convolution fusion | flops 2160066560 | bytes 11026432 | tf_op jit(solution)/shard_map/dot_general | solution.py:13
  9.6 0.0 copy-start.2
  9.6 41.2 %fusion.5 = f32[1024,4096]{1,0:T(8,128)S(1)} fusion(bf16[4096,4096]{1,0:T(8,128)(2,1)} %param.10, bf16[1024,4096]{1,0:T(8,128)(2,1)} %maximum_convert_fusion.clone.4), kind=kOutput, calls=%fused_computation.7 | convolution fusion | flops 34359738368 | bytes 58720256 | tf_op jit(solution)/shard_map/dot_general | solution.py:17
  50.8 0.0 copy-start.1
  50.8 0.0 copy-done.2
  50.8 15.7 %fusion = f32[1,1024]{1,0:T(1,128)S(1)} fusion(f32[4096,1]{0,1:T(1,128)} %bitcast.29, f32[1024,4096]{1,0:T(8,128)S(1)} %fusion.5, f32[4096]{0:T(1024)S(1)} %copy-done.2), kind=kOutput, calls=%fused_computation | convolution fusion | flops 58720256 | bytes 16814080 | tf_op jit(solution)/shard_map/dot_general | solution.py:23
  66.6 0.1 reshape.35
  66.6 0.2 convolution_convert_fusion.1
  66.8 0.7 copy.11
  67.6 7.3 %all-to-all-start.1 = ((bf16[32,2,32]{2,1,0:T(2,128)(2,1)}), bf16[32,2,32]{2,1,0:T(2,128)(2,1)S(1)}, u32[]{:S(2)}, u32[]{:S(2)}) async-start(bf16[32,2,32]{2,1,0:T(2,128)(2,1)} %bitcast.5), calls=%async_computation.1 | async-start | bytes 32768 | tf_op jit(solution)/shard_map/all_to_all | solution.py:46
  74.9 0.0 copy-done.1
  74.9 0.2 reshape.32
  75.2 0.4 convolution_convert_fusion
  75.6 1.2 %copy.13 = bf16[8,8,32,256]{3,2,1,0:T(8,128)(2,1)} copy(bf16[8,8,32,256]{3,1,2,0:T(8,128)(2,1)S(1)} %bitcast.26) | data formatting | bytes 2097152
  76.8 5.3 %all-to-all-done.1 = bf16[32,2,32]{2,1,0:T(2,128)(2,1)S(1)} async-done(((bf16[32,2,32]{2,1,0:T(2,128)(2,1)}), bf16[32,2,32]{2,1,0:T(2,128)(2,1)S(1)}, u32[]{:S(2)}, u32[]{:S(2)}) %all-to-all-start.1) | async-done | bytes 4128 | tf_op jit(solution)/shard_map/all_to_all | solution.py:46
  82.1 2.6 %all-to-all-start = ((bf16[32,2,32,256]{3,2,1,0:T(8,128)(2,1)}), bf16[32,2,32,256]{3,2,1,0:T(8,128)(2,1)S(1)}, u32[]{:S(2)}, u32[]{:S(2)}) async-start(bf16[32,2,32,256]{3,2,1,0:T(8,128)(2,1)} %bitcast.9), calls=%async_computation | async-start | bytes 2097152 | tf_op jit(solution)/shard_map/all_to_all | solution.py:45
  84.7 0.7 copy.12
  85.4 25.5 %all-to-all-done = bf16[32,2,32,256]{3,2,1,0:T(8,128)(2,1)S(1)} async-done(((bf16[32,2,32,256]{3,2,1,0:T(8,128)(2,1)}), bf16[32,2,32,256]{3,2,1,0:T(8,128)(2,1)S(1)}, u32[]{:S(2)}, u32[]{:S(2)}) %all-to-all-start) | async-done | bytes 1048608 | tf_op jit(solution)/shard_map/all_to_all | solution.py:45
  110.9 1.0 copy.15
Async XLA Ops:
  0.6 2.3 %copy-start = (bf16[256,4096]{1,0:T(8,128)(2,1)S(1)}, bf16[256,4096]{1,0:T(8,128)(2,1)}, u32[]{:S(2)}) copy-start(bf16[256,4096]{1,0:T(8,128)(2,1)} %param.8) | copy-start | bytes 6291460
  9.6 41.2 %copy-start.2 = (f32[4096]{0:T(1024)S(1)}, f32[4096]{0:T(1024)}, u32[]{:S(2)}) copy-start(f32[4096]{0:T(1024)} %param.11) | copy-start | bytes 49156
  50.8 24.1 %copy-start.1 = (bf16[1024,256]{1,0:T(8,128)(2,1)S(1)}, bf16[1024,256]{1,0:T(8,128)(2,1)}, u32[]{:S(2)}) copy-start(bf16[1024,256]{1,0:T(8,128)(2,1)} %param.7) | copy-start | bytes 1572868
  67.6 14.5 %all-to-all-start.1 = ((bf16[32,2,32]{2,1,0:T(2,128)(2,1)}), bf16[32,2,32]{2,1,0:T(2,128)(2,1)S(1)}, u32[]{:S(2)}, u32[]{:S(2)}) async-start(bf16[32,2,32]{2,1,0:T(2,128)(2,1)} %bitcast.5), calls=%async_computation.1 | async-start | bytes 32768 | tf_op jit(solution)/shard_map/all_to_all | solution.py:46
  82.1 28.8 %all-to-all-start = ((bf16[32,2,32,256]{3,2,1,0:T(8,128)(2,1)}), bf16[32,2,32,256]{3,2,1,0:T(8,128)(2,1)S(1)}, u32[]{:S(2)}, u32[]{:S(2)}) async-start(bf16[32,2,32,256]{3,2,1,0:T(8,128)(2,1)} %bitcast.9), calls=%async_computation | async-start | bytes 2097152 | tf_op jit(solution)/shard_map/all_to_all | solution.py:45
where the time goes:
time: 112 us
  matrix products  64.2 us (57%)
  waiting for transfers between devices  30.8 us (28%)
  starting transfers between devices  9.98 us (9%)
  local copies, waits for them, and re-layouts  3.94 us (4%)
  other arithmetic  2.3 us (2%)
    dot_general x1, matrix products, local(): jnp.dot(lax.all_gather(hidden, 'mp', axis=1, tiled=True), second_weight,...  41.2 us
    all_to_all x1, waiting for transfers between devices, local(): lax.all_to_all(outgoing, 'dp', split_axis=0, concat_axis=0, tiled=True)  25.5 us
    dot_general x1, matrix products, local(): jnp.dot(hidden_two, head_weight, precision=lax.Precision.HIGHEST)  15.7 us
    all_to_all x1, starting transfers between devices, local(): lax.all_to_all(outgoing_scores, 'dp', split_axis=0, concat_axis=0, tiled=...  7.33 us
    dot_general x1, matrix products, local(): jnp.dot(full_rows, first_weight, preferred_element_type=jnp.float32)  6.61 us
    all_to_all x1, waiting for transfers between devices, local(): lax.all_to_all(outgoing_scores, 'dp', split_axis=0, concat_axis=0, tiled=...  5.27 us
    unnamed x9, local copies, waits for them, and re-layouts  2.9 us
    all_to_all x1, starting transfers between devices, local(): lax.all_to_all(outgoing, 'dp', split_axis=0, concat_axis=0, tiled=True)  2.65 us
  transfers between devices with their start and end apart: 2, of which 2 were waited for; matrix products, arithmetic and copies ran while one was open for 2% of the time, Pallas kernels for 0%

commit v1 on v0

--- a/solution.py
+++ b/solution.py
@@ -1,13 +1,170 @@
+import functools
+
 import jax
 import jax.numpy as jnp
 from jax import lax
+from jax.experimental import pallas as pl
+from jax.experimental.pallas import tpu as pltpu
 from jax.sharding import PartitionSpec as P
+
 
 BROWS = 32
 PAIR = 2
+LANES = 128
+
+
+def route_kernel(owners_ref, blocks_ref, out_ref, source_ref):
+    block_count = blocks_ref.shape[0]
+    slot_count = out_ref.shape[0]
+    for s in range(slot_count):
+        source_ref[s] = -1
+    for b in range(block_count):
+        first = owners_ref[b] * PAIR
+        slot = first + jnp.where(source_ref[first] >= 0, 1, 0)
+        source_ref[slot] = b
+
+    def place(s, carry):
+        source = source_ref[s]
+        rows = blocks_ref[jnp.maximum(source, 0)]
+        out_ref[s] = jnp.where(source >= 0, rows, jnp.zeros_like(rows))
+        return carry
+
+    lax.fori_loop(0, slot_count, place, 0, unroll=8)
+
+
+def route(owner_list, candidates, collectors):
+    rows, width = candidates.shape
+    blocks = candidates.reshape(rows // BROWS, BROWS, width)
+    slots = collectors * PAIR
+    return pl.pallas_call(
+        route_kernel,
+        out_shape=jax.ShapeDtypeStruct((slots, BROWS, width), candidates.dtype),
+        in_specs=[
+            pl.BlockSpec(memory_space=pltpu.SMEM),
+            pl.BlockSpec(memory_space=pltpu.VMEM),
+        ],
+        out_specs=pl.BlockSpec(memory_space=pltpu.VMEM),
+        scratch_shapes=[pltpu.SMEM((slots,), jnp.int32)],
+        name="route",
+    )(owner_list, blocks)
+
+
+def score_kernel(
+    x_ref, w1_ref, b1_ref, w2_ref, b2_ref, head_ref, column_ref, row_ref,
+    out_ref, hidden_ref, sums_ref, *, tile_m, tile_h,
+):
+    rows = x_ref.shape[0]
+    width = w1_ref.shape[1]
+    tile_n = w2_ref.shape[1]
+    step = pl.program_id(0)
+
+    @pl.when(step == 0)
+    def _():
+        sums_ref[...] = jnp.zeros_like(sums_ref)
+
+        def first_layer(i, carry):
+            at = pl.ds(pl.multiple_of(i * tile_h, tile_h), tile_h)
+            first = jnp.dot(x_ref[...], w1_ref[:, at], preferred_element_type=jnp.float32)
+            first = first + b1_ref[:, at].astype(jnp.float32)
+            hidden_ref[:, at] = jnp.maximum(first, 0.0).astype(jnp.bfloat16)
+            return carry
+
+        lax.fori_loop(0, width // tile_h, first_layer, 0)
+
+    for m in range(rows // tile_m):
+        at = pl.ds(m * tile_m, tile_m)
+        second = jnp.dot(hidden_ref[at, :], w2_ref[...], preferred_element_type=jnp.float32)
+        weighted = jnp.maximum(second + b2_ref[...], 0.0) * head_ref[...]
+        total = weighted[:, :LANES]
+        for q in range(1, tile_n // LANES):
+            total = total + weighted[:, q * LANES:(q + 1) * LANES]
+        sums_ref[at, :] += total
+
+    @pl.when(step == pl.num_programs(0) - 1)
+    def _():
+        blocks = rows // BROWS
+        scores = jnp.sum(sums_ref[...].reshape(blocks, BROWS, LANES), axis=2)
+        rounded = scores.astype(jnp.bfloat16)
+        owner_row = row_ref[...]
+        same_owner = column_ref[...] == owner_row
+        before = lax.broadcasted_iota(jnp.int32, (blocks, blocks), 0) < lax.broadcasted_iota(
+            jnp.int32, (blocks, blocks), 1
+        )
+        rank = jnp.sum(jnp.where(same_owner & before, 1, 0), axis=0, keepdims=True)
+        target = owner_row * PAIR + rank
+        collectors = out_ref.shape[0]
+        for k in range(PAIR):
+            slot = lax.broadcasted_iota(jnp.int32, (collectors, blocks), 0) * PAIR + k
+            chooser = jnp.where(slot == target, 1.0, 0.0).astype(jnp.bfloat16)
+            placed = jnp.dot(chooser, rounded, preferred_element_type=jnp.float32)
+            out_ref[:, k, :] = placed.astype(out_ref.dtype)
+
+
+def score(candidates, first_weight, first_bias, second_weight, second_bias, head_weight, owners, collectors):
+    rows, domains = candidates.shape
+    width = first_weight.shape[1]
+    outs = second_weight.shape[1]
+    blocks = owners.shape[0]
+    tile_n, tile_m, tile_h = 512, 512, 512
+
+    def whole(*shape):
+        return pl.BlockSpec(shape, lambda j: (0,) * len(shape), pipeline_mode=pl.Buffered(1))
+
+    return pl.pallas_call(
+        functools.partial(score_kernel, tile_m=tile_m, tile_h=tile_h),
+        out_shape=jax.ShapeDtypeStruct((collectors, PAIR, BROWS), jnp.bfloat16),
+        grid=(outs // tile_n,),
+        in_specs=[
+            whole(rows, domains),
+            whole(domains, width),
+            whole(1, width),
+            pl.BlockSpec((width, tile_n), lambda j: (0, j)),
+            pl.BlockSpec((1, tile_n), lambda j: (0, j)),
+            pl.BlockSpec((1, tile_n), lambda j: (0, j)),
+            whole(blocks, 1),
+            whole(1, blocks),
+        ],
+        out_specs=pl.BlockSpec((collectors, PAIR, BROWS), lambda j: (0, 0, 0)),
+        scratch_shapes=[
+            pltpu.VMEM((rows, width), jnp.bfloat16),
+            pltpu.VMEM((rows, LANES), jnp.float32),
+        ],
+        compiler_params=pltpu.CompilerParams(vmem_limit_bytes=40 << 20),
+        cost_estimate=pl.CostEstimate(
+            flops=2 * rows * width * (domains + outs),
+            transcendentals=0,
+            bytes_accessed=2 * (rows * domains + domains * width + width * outs),
+        ),
+        name="score",
+    )(
+        candidates, first_weight, first_bias, second_weight, second_bias.reshape(1, -1),
+        head_weight.reshape(1, -1), owners, owners.reshape(1, -1),
+    )
 
 
 def local(candidates, first_weight, first_bias, second_weight, second_bias, head_weight, owners):
+    if lax.axis_size("mp") > 1:
+        return split_local(
+            candidates, first_weight, first_bias, second_weight, second_bias, head_weight, owners
+        )
+    collectors = lax.axis_size("dp")
+    width = candidates.shape[1]
+    outgoing = route(owners[:, 0], candidates, collectors)
+    outgoing = outgoing.reshape(collectors, PAIR, BROWS, width)
+    arrived = lax.all_to_all(outgoing, "dp", split_axis=0, concat_axis=0, tiled=True)
+    outgoing_scores = score(
+        candidates, first_weight, first_bias, second_weight, second_bias, head_weight, owners,
+        collectors,
+    )
+    arrived, outgoing_scores = lax.optimization_barrier((arrived, outgoing_scores))
+    arrived_scores = lax.all_to_all(outgoing_scores, "dp", split_axis=0, concat_axis=0, tiled=True)
+    return (
+        arrived.reshape(collectors * PAIR, BROWS, width),
+        arrived_scores.reshape(collectors * PAIR, BROWS),
+    )
+
+
+def split_local(candidates, first_weight, first_bias, second_weight, second_bias, head_weight, owners):
     slice_width = candidates.shape[1]
     full_rows = lax.all_gather(candidates, "mp", axis=1, tiled=True)
     first_local = jnp.dot(

time: 112 us -> 74.7 us (0.67)
  matrix products: 64.2 us -> 0 us
  Pallas kernels: 0 us -> 45.4 us
  waiting for transfers between devices: 30.8 us -> 7.18 us
  local copies, waits for them, and re-layouts: 3.94 us -> 7.83 us
  starting transfers between devices: 9.98 us -> 13.2 us
  other arithmetic: 2.3 us -> 0 us
    dot_general x5 -> x0, matrix products: 64.2 us -> none  [the longest x1 41.2 us: local(): jnp.dot(lax.all_gather(hidden, 'mp', axis=1, tiled=True), second_weight,...]
    pallas_call x0 -> x2, Pallas kernels: none -> 45.4 us  [the longest x1 42.9 us: score(): pl.pallas_call(functools.partial(score_kernel, tile_m=tile_m, tile_h=tile...]
    all_to_all x1, waiting for transfers between devices: 25.5 us -> 0.01 us  [local(): lax.all_to_all(outgoing, 'dp', split_axis=0, concat_axis=0, tiled=True)]
    unnamed x9 -> x15, local copies, waits for them, and re-layouts: 2.9 us -> 7.83 us
    all_to_all x1, starting transfers between devices: 2.65 us -> 7.33 us  [local(): lax.all_to_all(outgoing, 'dp', split_axis=0, concat_axis=0, tiled=True)]
    all_to_all x1, waiting for transfers between devices: 5.27 us -> 7.17 us  [local(): lax.all_to_all(outgoing_scores, 'dp', split_axis=0, concat_axis=0, tiled=...]
    all_to_all x1, starting transfers between devices: 7.33 us -> 5.83 us  [local(): lax.all_to_all(outgoing_scores, 'dp', split_axis=0, concat_axis=0, tiled=...]
    add x2 -> x0, other arithmetic: 1.39 us -> none  [the longest x1 0.73 us: local(): jnp.dot(full_rows, first_weight, preferred_element_type=jnp.float32)]
  transfers between devices with their start and end apart: 2 -> 2, of which waited for: 2 -> 1; matrix products, arithmetic and copies ran while one was open for 2% -> 1% of each run, Pallas kernels for 0% -> 58%
where the time goes in v1:
time: 74.7 us; the launch traced here: 74.2 us
  Pallas kernels  45.4 us (61%)
  starting transfers between devices  13.2 us (18%)
  local copies, waits for them, and re-layouts  7.83 us (10%)
  waiting for transfers between devices  7.18 us (10%)
    pallas_call x1, Pallas kernels, score(): pl.pallas_call(functools.partial(score_kernel, tile_m=tile_m, tile_h=tile...  42.9 us
    unnamed x15, local copies, waits for them, and re-layouts  7.83 us
    all_to_all x1, starting transfers between devices, local(): lax.all_to_all(outgoing, 'dp', split_axis=0, concat_axis=0, tiled=True)  7.33 us
    all_to_all x1, waiting for transfers between devices, local(): lax.all_to_all(outgoing_scores, 'dp', split_axis=0, concat_axis=0, tiled=...  7.17 us
    all_to_all x1, starting transfers between devices, local(): lax.all_to_all(outgoing_scores, 'dp', split_axis=0, concat_axis=0, tiled=...  5.83 us
    pallas_call x1, Pallas kernels, route(): pl.pallas_call(route_kernel, out_shape=jax.ShapeDtypeStruct((slots, BROWS...  2.47 us
  transfers between devices with their start and end apart: 2, of which 1 were waited for; matrix products, arithmetic and copies ran while one was open for 1% of the time, Pallas kernels for 58%

profile of v1, /device:TPU:0, one launch (start us, length us, event | category | flops | bytes accessed | tf_op | source)
XLA Modules:
  0.0 74.2 jit_solution(11488643651173370317)
XLA Ops:
  0.6 2.5 %route.1 = bf16[64,32,256]{2,1,0:T(8,128)(2,1)} custom-call(s32[32]{0:T(128)} %bitcast.9, bf16[32,32,256]{2,1,0:T(8,128)(2,1)} %bitcast.8), custom_call_target="tpu_custom_call" | custom-call | tf_op jit(solution)/shard_map/route/pallas_call | solution.py:39
  3.1 7.3 %all-to-all-start = ((bf16[32,2,32,256]{3,2,1,0:T(8,128)(2,1)}), bf16[32,2,32,256]{3,2,1,0:T(8,128)(2,1)S(1)}, u32[]{:S(2)}, u32[]{:S(2)}) async-start(bf16[32,2,32,256]{3,2,1,0:T(8,128)(2,1)} %bitcast.14), calls=%async_computation | async-start | bytes 2097152 | tf_op jit(solution)/shard_map/all_to_all | solution.py:154
  10.4 0.7 copy.9.column_ref
  11.2 0.0 copy-start
  11.2 1.0 %copy-done = bf16[1024,256]{1,0:T(8,128)(2,1)S(1)} copy-done((bf16[1024,256]{1,0:T(8,128)(2,1)S(1)}, bf16[1024,256]{1,0:T(8,128)(2,1)}, u32[]{:S(2)}) %copy-start) | copy-done | bytes 524312
  12.2 0.0 copy-start.1
  12.2 0.7 copy-done.1
  12.9 0.0 copy-start.2
  12.9 1.6 %copy-done.2 = bf16[256,4096]{1,0:T(8,128)(2,1)S(1)} copy-done((bf16[256,4096]{1,0:T(8,128)(2,1)S(1)}, bf16[256,4096]{1,0:T(8,128)(2,1)}, u32[]{:S(2)}) %copy-start.2) | copy-done | bytes 2097176
  14.5 0.0 copy-start.3
  14.5 0.7 copy-done.3
  15.2 0.0 copy-start.4
  15.2 0.7 copy-done.4
  15.9 0.0 copy-start.5
  15.9 0.7 copy-done.5
  16.6 42.9 %score.1 = bf16[32,2,32]{2,1,0:T(2,128)(2,1)} custom-call(bf16[1024,256]{1,0:T(8,128)(2,1)S(1)} %copy-done, bf16[256,4096]{1,0:T(8,128)(2,1)S(1)} %copy-done.2, bf16[1,4096]{1,0:T(2,128)(2,1)S(1)} %copy-done.3, bf16[4096,4096]{1,0:T(8,128)(2,1)} %w2_ref.1, f32[1,4096]{1,0:T(1,128)S(1)} %bitcast.11, f32[1,4096]{1,0:T(1,128)S(1)} %bitcast.12, ...), custom_call_target="tpu_custom_call" | custom-call | flops 36507222016 | bytes 36175872 | tf_op jit(solution)/shard_map/score/pallas_call | solution.py:113
  59.5 0.0 all-to-all-done
  59.5 5.8 %all-to-all-start.1 = ((bf16[32,2,32]{2,1,0:T(2,128)(2,1)}), bf16[32,2,32]{2,1,0:T(2,128)(2,1)S(1)}, u32[]{:S(2)}, u32[]{:S(2)}) async-start(bf16[32,2,32]{2,1,0:T(2,128)(2,1)} %score.1), calls=%async_computation.1 | async-start | bytes 32768 | tf_op jit(solution)/shard_map/all_to_all | solution.py:160
  65.4 7.2 %all-to-all-done.1 = bf16[32,2,32]{2,1,0:T(2,128)(2,1)S(1)} async-done(((bf16[32,2,32]{2,1,0:T(2,128)(2,1)}), bf16[32,2,32]{2,1,0:T(2,128)(2,1)S(1)}, u32[]{:S(2)}, u32[]{:S(2)}) %all-to-all-start.1) | async-done | bytes 4128 | tf_op jit(solution)/shard_map/all_to_all | solution.py:160
  72.5 0.7 copy.10
  73.2 1.0 %copy.12 = bf16[64,32,256]{2,1,0:T(8,128)(2,1)} copy(bf16[64,32,256]{2,1,0:T(8,128)(2,1)S(1)} %bitcast.13) | data formatting | bytes 2097152
Async XLA Ops:
  3.1 56.4 %all-to-all-start = ((bf16[32,2,32,256]{3,2,1,0:T(8,128)(2,1)}), bf16[32,2,32,256]{3,2,1,0:T(8,128)(2,1)S(1)}, u32[]{:S(2)}, u32[]{:S(2)}) async-start(bf16[32,2,32,256]{3,2,1,0:T(8,128)(2,1)} %bitcast.14), calls=%async_computation | async-start | bytes 2097152 | tf_op jit(solution)/shard_map/all_to_all | solution.py:154
  11.2 1.0 %copy-start = (bf16[1024,256]{1,0:T(8,128)(2,1)S(1)}, bf16[1024,256]{1,0:T(8,128)(2,1)}, u32[]{:S(2)}) copy-start(bf16[1024,256]{1,0:T(8,128)(2,1)} %x_ref.1) | copy-start | bytes 1572868
  12.2 0.7 copy-start.1
  12.9 1.6 %copy-start.2 = (bf16[256,4096]{1,0:T(8,128)(2,1)S(1)}, bf16[256,4096]{1,0:T(8,128)(2,1)}, u32[]{:S(2)}) copy-start(bf16[256,4096]{1,0:T(8,128)(2,1)} %w1_ref.1) | copy-start | bytes 6291460
  14.5 0.7 copy-start.3
  15.2 0.7 copy-start.4
  15.9 0.7 copy-start.5
  59.5 13.0 %all-to-all-start.1 = ((bf16[32,2,32]{2,1,0:T(2,128)(2,1)}), bf16[32,2,32]{2,1,0:T(2,128)(2,1)S(1)}, u32[]{:S(2)}, u32[]{:S(2)}) async-start(bf16[32,2,32]{2,1,0:T(2,128)(2,1)} %score.1), calls=%async_computation.1 | async-start | bytes 32768 | tf_op jit(solution)/shard_map/all_to_all | solution.py:160

commit v2 on v1

--- a/solution.py
+++ b/solution.py
@@ -11,6 +11,7 @@
 BROWS = 32
 PAIR = 2
 LANES = 128
+VMEM_GRANT = (64 << 20) - (512 << 10)
 
 
 def route_kernel(owners_ref, blocks_ref, out_ref, source_ref):
@@ -50,54 +51,89 @@
 
 
 def score_kernel(
-    x_ref, w1_ref, b1_ref, w2_ref, b2_ref, head_ref, column_ref, row_ref,
-    out_ref, hidden_ref, sums_ref, *, tile_m, tile_h,
+    x_hbm, w1_hbm, b1_hbm, w2_hbm, b2_hbm, head_hbm, owners_hbm, out_ref,
+    x_ref, w1_ref, b1_ref, w2_ref, b2_ref, head_ref, owners_ref, hidden_ref, sums_ref, chooser_ref,
+    small_sem, w1_sem, w2_sem, *, tile_m, tile_h,
 ):
     rows = x_ref.shape[0]
     width = w1_ref.shape[1]
-    tile_n = w2_ref.shape[1]
-    step = pl.program_id(0)
-
-    @pl.when(step == 0)
-    def _():
-        sums_ref[...] = jnp.zeros_like(sums_ref)
-
-        def first_layer(i, carry):
-            at = pl.ds(pl.multiple_of(i * tile_h, tile_h), tile_h)
+    slots, _, tile_n = w2_ref.shape
+    tiles = w2_hbm.shape[1] // tile_n
+    first_tiles = w1_sem.shape[0]
+    columns = width // first_tiles
+    blocks = rows // BROWS
+    collectors = out_ref.shape[0]
+
+    pairs = (
+        (owners_hbm, owners_ref), (x_hbm, x_ref), (b1_hbm, b1_ref), (b2_hbm, b2_ref), (head_hbm, head_ref)
+    )
+    small = [pltpu.make_async_copy(a, b, small_sem.at[i]) for i, (a, b) in enumerate(pairs)]
+    firsts = [
+        pltpu.make_async_copy(
+            w1_hbm.at[:, pl.ds(i * columns, columns)], w1_ref.at[:, pl.ds(i * columns, columns)], w1_sem.at[i]
+        )
+        for i in range(first_tiles)
+    ]
+
+    def load(j):
+        at = pl.ds(pl.multiple_of(j * tile_n, tile_n), tile_n)
+        return pltpu.make_async_copy(w2_hbm.at[:, at], w2_ref.at[j % slots], w2_sem.at[j % slots])
+
+    for copy in small[:3] + firsts + small[3:]:
+        copy.start()
+
+    sums_ref[...] = jnp.zeros_like(sums_ref)
+    small[0].wait()
+    owner_row = jnp.broadcast_to(owners_ref[...], (blocks, blocks)).astype(jnp.float32)
+    same_owner = owner_row == jnp.transpose(owner_row)
+    before = lax.broadcasted_iota(jnp.int32, (blocks, blocks), 0) < lax.broadcasted_iota(
+        jnp.int32, (blocks, blocks), 1
+    )
+    rank = jnp.sum(jnp.where(same_owner & before, 1.0, 0.0), axis=0, keepdims=True)
+    target = owner_row[:1] * PAIR + rank
+    for k in range(PAIR):
+        slot = lax.broadcasted_iota(jnp.int32, (collectors, blocks), 0) * PAIR + k
+        chooser_ref[k] = jnp.where(slot.astype(jnp.float32) == target, 1.0, 0.0).astype(jnp.bfloat16)
+
+    small[1].wait()
+    small[2].wait()
+    for i, copy in enumerate(firsts):
+        copy.wait()
+        if i == 0:
+            load(0).start()
+        for q in range(columns // tile_h):
+            at = pl.ds(i * columns + q * tile_h, tile_h)
             first = jnp.dot(x_ref[...], w1_ref[:, at], preferred_element_type=jnp.float32)
             first = first + b1_ref[:, at].astype(jnp.float32)
             hidden_ref[:, at] = jnp.maximum(first, 0.0).astype(jnp.bfloat16)
-            return carry
-
-        lax.fori_loop(0, width // tile_h, first_layer, 0)
-
-    for m in range(rows // tile_m):
-        at = pl.ds(m * tile_m, tile_m)
-        second = jnp.dot(hidden_ref[at, :], w2_ref[...], preferred_element_type=jnp.float32)
-        weighted = jnp.maximum(second + b2_ref[...], 0.0) * head_ref[...]
-        total = weighted[:, :LANES]
-        for q in range(1, tile_n // LANES):
-            total = total + weighted[:, q * LANES:(q + 1) * LANES]
-        sums_ref[at, :] += total
-
-    @pl.when(step == pl.num_programs(0) - 1)
-    def _():
-        blocks = rows // BROWS
-        scores = jnp.sum(sums_ref[...].reshape(blocks, BROWS, LANES), axis=2)
-        rounded = scores.astype(jnp.bfloat16)
-        owner_row = row_ref[...]
-        same_owner = column_ref[...] == owner_row
-        before = lax.broadcasted_iota(jnp.int32, (blocks, blocks), 0) < lax.broadcasted_iota(
-            jnp.int32, (blocks, blocks), 1
-        )
-        rank = jnp.sum(jnp.where(same_owner & before, 1, 0), axis=0, keepdims=True)
-        target = owner_row * PAIR + rank
-        collectors = out_ref.shape[0]
-        for k in range(PAIR):
-            slot = lax.broadcasted_iota(jnp.int32, (collectors, blocks), 0) * PAIR + k
-            chooser = jnp.where(slot == target, 1.0, 0.0).astype(jnp.bfloat16)
-            placed = jnp.dot(chooser, rounded, preferred_element_type=jnp.float32)
-            out_ref[:, k, :] = placed.astype(out_ref.dtype)
+    small[3].wait()
+    small[4].wait()
+
+    def second_layer(j, carry):
+        load(j).wait()
+
+        @pl.when(j + 1 < tiles)
+        def _():
+            load(j + 1).start()
+
+        columns_at = pl.ds(pl.multiple_of(j * tile_n, tile_n), tile_n)
+        for m in range(rows // tile_m):
+            at = pl.ds(m * tile_m, tile_m)
+            second = jnp.dot(hidden_ref[at, :], w2_ref[j % slots], preferred_element_type=jnp.float32)
+            weighted = jnp.maximum(second + b2_ref[:, columns_at], 0.0) * head_ref[:, columns_at]
+            total = weighted[:, :LANES]
+            for q in range(1, tile_n // LANES):
+                total = total + weighted[:, q * LANES:(q + 1) * LANES]
+            sums_ref[at, :] += total
+        return carry
+
+    lax.fori_loop(0, tiles, second_layer, 0)
+
+    scores = jnp.sum(sums_ref[...].reshape(blocks, BROWS, LANES), axis=2)
+    rounded = scores.astype(jnp.bfloat16)
+    for k in range(PAIR):
+        placed = jnp.dot(chooser_ref[k], rounded, preferred_element_type=jnp.float32)
+        out_ref[:, k, :] = placed.astype(out_ref.dtype)
 
 
 def score(candidates, first_weight, first_bias, second_weight, second_bias, head_weight, owners, collectors):
@@ -105,31 +141,28 @@
     width = first_weight.shape[1]
     outs = second_weight.shape[1]
     blocks = owners.shape[0]
-    tile_n, tile_m, tile_h = 512, 512, 512
-
-    def whole(*shape):
-        return pl.BlockSpec(shape, lambda j: (0,) * len(shape), pipeline_mode=pl.Buffered(1))
-
+    tile_n, tile_m, tile_h, first_tiles, slots = 512, 512, 512, 4, 2
     return pl.pallas_call(
         functools.partial(score_kernel, tile_m=tile_m, tile_h=tile_h),
         out_shape=jax.ShapeDtypeStruct((collectors, PAIR, BROWS), jnp.bfloat16),
-        grid=(outs // tile_n,),
-        in_specs=[
-            whole(rows, domains),
-            whole(domains, width),
-            whole(1, width),
-            pl.BlockSpec((width, tile_n), lambda j: (0, j)),
-            pl.BlockSpec((1, tile_n), lambda j: (0, j)),
-            pl.BlockSpec((1, tile_n), lambda j: (0, j)),
-            whole(blocks, 1),
-            whole(1, blocks),
-        ],
-        out_specs=pl.BlockSpec((collectors, PAIR, BROWS), lambda j: (0, 0, 0)),
+        in_specs=[pl.BlockSpec(memory_space=pltpu.HBM)] * 7,
+        out_specs=pl.BlockSpec(memory_space=pltpu.VMEM),
         scratch_shapes=[
+            pltpu.VMEM((rows, domains), candidates.dtype),
+            pltpu.VMEM((domains, width), first_weight.dtype),
+            pltpu.VMEM((1, width), first_bias.dtype),
+            pltpu.VMEM((slots, width, tile_n), second_weight.dtype),
+            pltpu.VMEM((1, outs), second_bias.dtype),
+            pltpu.VMEM((1, outs), head_weight.dtype),
+            pltpu.VMEM((1, blocks), owners.dtype),
             pltpu.VMEM((rows, width), jnp.bfloat16),
             pltpu.VMEM((rows, LANES), jnp.float32),
+            pltpu.VMEM((PAIR, collectors, blocks), jnp.bfloat16),
+            pltpu.SemaphoreType.DMA((5,)),
+            pltpu.SemaphoreType.DMA((first_tiles,)),
+            pltpu.SemaphoreType.DMA((slots,)),
         ],
-        compiler_params=pltpu.CompilerParams(vmem_limit_bytes=40 << 20),
+        compiler_params=pltpu.CompilerParams(vmem_limit_bytes=VMEM_GRANT),
         cost_estimate=pl.CostEstimate(
             flops=2 * rows * width * (domains + outs),
             transcendentals=0,
@@ -138,8 +171,32 @@
         name="score",
     )(
         candidates, first_weight, first_bias, second_weight, second_bias.reshape(1, -1),
-        head_weight.reshape(1, -1), owners, owners.reshape(1, -1),
-    )
+        head_weight.reshape(1, -1), owners.reshape(1, -1),
+    )
+
+
+def settle_kernel(arrived_hbm, out_hbm, sems):
+    parts = sems.shape[0]
+    size = arrived_hbm.shape[0] // parts
+    copies = [
+        pltpu.make_async_copy(arrived_hbm.at[pl.ds(i * size, size)], out_hbm.at[pl.ds(i * size, size)], sems.at[i])
+        for i in range(parts)
+    ]
+    for copy in copies:
+        copy.start()
+    for copy in copies:
+        copy.wait()
+
+
+def settle(arrived):
+    return pl.pallas_call(
+        settle_kernel,
+        out_shape=jax.ShapeDtypeStruct(arrived.shape, arrived.dtype),
+        in_specs=[pl.BlockSpec(memory_space=pltpu.HBM)],
+        out_specs=pl.BlockSpec(memory_space=pltpu.HBM),
+        scratch_shapes=[pltpu.SemaphoreType.DMA((8 if arrived.shape[0] % 8 == 0 else 1,))],
+        name="settle",
+    )(arrived)
 
 
 def local(candidates, first_weight, first_bias, second_weight, second_bias, head_weight, owners):
@@ -158,8 +215,9 @@
     )
     arrived, outgoing_scores = lax.optimization_barrier((arrived, outgoing_scores))
     arrived_scores = lax.all_to_all(outgoing_scores, "dp", split_axis=0, concat_axis=0, tiled=True)
+    collected = settle(arrived.reshape(collectors * PAIR, BROWS, width))
     return (
-        arrived.reshape(collectors * PAIR, BROWS, width),
+        collected,
         arrived_scores.reshape(collectors * PAIR, BROWS),
     )
 

time: 74.7 us -> 91.5 us (1.22)
  Pallas kernels: 45.4 us -> 76.6 us
  waiting for transfers between devices: 7.18 us -> 0.01 us
  local copies, waits for them, and re-layouts: 7.83 us -> 0.68 us
    pallas_call x0 -> x1, Pallas kernels: none -> 32.9 us  [settle(): pl.pallas_call(settle_kernel, out_shape=jax.ShapeDtypeStruct(arrived.shap...]
    all_to_all x1, waiting for transfers between devices: 7.17 us -> 0.01 us  [local(): lax.all_to_all(outgoing_scores, 'dp', split_axis=0, concat_axis=0, tiled=...]
    unnamed x15 -> x1, local copies, waits for them, and re-layouts: 7.83 us -> 0.68 us
    pallas_call x1, Pallas kernels: 42.9 us -> 41.2 us  [score(): pl.pallas_call(functools.partial(score_kernel, tile_m=tile_m, tile_h=tile...]
  transfers between devices with their start and end apart: 2 -> 2, of which waited for: 1 -> 0; matrix products, arithmetic and copies ran while one was open for 1% -> 0% of each run, Pallas kernels for 58% -> 81%
where the time goes in v2:
time: 91.5 us; the launch traced here: 91.2 us
  Pallas kernels  76.6 us (84%)
  starting transfers between devices  13.2 us (14%)
    pallas_call x1, Pallas kernels, score(): pl.pallas_call(functools.partial(score_kernel, tile_m=tile_m, tile_h=tile...  41.2 us
    pallas_call x1, Pallas kernels, settle(): pl.pallas_call(settle_kernel, out_shape=jax.ShapeDtypeStruct(arrived.shap...  32.9 us
    all_to_all x1, starting transfers between devices, local(): lax.all_to_all(outgoing, 'dp', split_axis=0, concat_axis=0, tiled=True)  7.45 us
    all_to_all x1, starting transfers between devices, local(): lax.all_to_all(outgoing_scores, 'dp', split_axis=0, concat_axis=0, tiled=...  5.76 us
    pallas_call x1, Pallas kernels, route(): pl.pallas_call(route_kernel, out_shape=jax.ShapeDtypeStruct((slots, BROWS...  2.47 us
  transfers between devices with their start and end apart: 2, of which 0 were waited for; matrix products, arithmetic and copies ran while one was open for 0% of the time, Pallas kernels for 81%

profile of v2, /device:TPU:0, one launch (start us, length us, event | category | flops | bytes accessed | tf_op | source)
XLA Modules:
  0.0 91.2 jit_solution(17554966047742605707)
XLA Ops:
  0.6 2.5 %route.1 = bf16[64,32,256]{2,1,0:T(8,128)(2,1)} custom-call(s32[32]{0:T(128)} %bitcast.11, bf16[32,32,256]{2,1,0:T(8,128)(2,1)} %bitcast.9), custom_call_target="tpu_custom_call" | custom-call | tf_op jit(solution)/shard_map/route/pallas_call | solution.py:40
  3.1 7.5 %all-to-all-start = ((bf16[32,2,32,256]{3,2,1,0:T(8,128)(2,1)}), bf16[32,2,32,256]{3,2,1,0:T(8,128)(2,1)}, u32[]{:S(2)}, u32[]{:S(2)}) async-start(bf16[32,2,32,256]{3,2,1,0:T(8,128)(2,1)} %bitcast.8), calls=%async_computation | async-start | bytes 2097152 | tf_op jit(solution)/shard_map/all_to_all | solution.py:211
  10.6 41.2 %score.1 = bf16[32,2,32]{2,1,0:T(2,128)(2,1)} custom-call(bf16[1024,256]{1,0:T(8,128)(2,1)} %x_hbm.1, bf16[256,4096]{1,0:T(8,128)(2,1)} %w1_hbm.1, bf16[1,4096]{1,0:T(2,128)(2,1)} %b1_hbm.1, bf16[4096,4096]{1,0:T(8,128)(2,1)} %w2_hbm.1, f32[1,4096]{1,0:T(1,128)} %bitcast.13, f32[1,4096]{1,0:T(1,128)} %bitcast.14, s32[1,32]{1,0:T(1,128)} %bitcast.12), custom_call_target="tpu_custom_call" | custom-call | flops 36507222016 | bytes 36175872 | tf_op jit(solution)/shard_map/score/pallas_call | solution.py:145
  51.8 0.0 all-to-all-done
  51.8 5.8 %all-to-all-start.1 = ((bf16[32,2,32]{2,1,0:T(2,128)(2,1)}), bf16[32,2,32]{2,1,0:T(2,128)(2,1)S(1)}, u32[]{:S(2)}, u32[]{:S(2)}) async-start(bf16[32,2,32]{2,1,0:T(2,128)(2,1)} %score.1), calls=%async_computation.1 | async-start | bytes 32768 | tf_op jit(solution)/shard_map/all_to_all | solution.py:217
  57.6 32.9 %settle.1 = bf16[64,32,256]{2,1,0:T(8,128)(2,1)} custom-call(bf16[64,32,256]{2,1,0:T(8,128)(2,1)} %bitcast.6.arrived_hbm), custom_call_target="tpu_custom_call" | custom-call | tf_op jit(solution)/shard_map/settle/pallas_call | solution.py:192
  90.5 0.0 all-to-all-done.1
  90.5 0.7 copy.9
Async XLA Ops:
  3.1 48.7 %all-to-all-start = ((bf16[32,2,32,256]{3,2,1,0:T(8,128)(2,1)}), bf16[32,2,32,256]{3,2,1,0:T(8,128)(2,1)}, u32[]{:S(2)}, u32[]{:S(2)}) async-start(bf16[32,2,32,256]{3,2,1,0:T(8,128)(2,1)} %bitcast.8), calls=%async_computation | async-start | bytes 2097152 | tf_op jit(solution)/shard_map/all_to_all | solution.py:211
  51.8 38.7 %all-to-all-start.1 = ((bf16[32,2,32]{2,1,0:T(2,128)(2,1)}), bf16[32,2,32]{2,1,0:T(2,128)(2,1)S(1)}, u32[]{:S(2)}, u32[]{:S(2)}) async-start(bf16[32,2,32]{2,1,0:T(2,128)(2,1)} %score.1), calls=%async_computation.1 | async-start | bytes 32768 | tf_op jit(solution)/shard_map/all_to_all | solution.py:217

commit v3 on v2

--- a/solution.py
+++ b/solution.py
@@ -11,79 +11,101 @@
 BROWS = 32
 PAIR = 2
 LANES = 128
-VMEM_GRANT = (64 << 20) - (512 << 10)
-
-
-def route_kernel(owners_ref, blocks_ref, out_ref, source_ref):
-    block_count = blocks_ref.shape[0]
-    slot_count = out_ref.shape[0]
+VMEM_GRANT = 36 << 20
+
+
+def route_kernel(
+    owners_ref, x_hbm, w1_hbm, b1_hbm, b2_hbm, head_hbm, row_hbm,
+    out_hbm, x_ref, w1_ref, b1_ref, b2_ref, head_ref, row_ref,
+    placed_ref, source_ref, in_sems, out_sems,
+):
+    parts = out_sems.shape[0]
+    slot_count = placed_ref.shape[0]
+    block_count = owners_ref.shape[0]
+    copies = [
+        pltpu.make_async_copy(a, b, in_sems.at[i])
+        for i, (a, b) in enumerate(
+            (
+                (x_hbm, x_ref), (w1_hbm, w1_ref), (b1_hbm, b1_ref), (b2_hbm, b2_ref), (head_hbm, head_ref),
+                (row_hbm, row_ref),
+            )
+        )
+    ]
+    for copy in copies:
+        copy.start()
     for s in range(slot_count):
         source_ref[s] = -1
     for b in range(block_count):
         first = owners_ref[b] * PAIR
         slot = first + jnp.where(source_ref[first] >= 0, 1, 0)
         source_ref[slot] = b
+    copies[0].wait()
 
     def place(s, carry):
         source = source_ref[s]
-        rows = blocks_ref[jnp.maximum(source, 0)]
-        out_ref[s] = jnp.where(source >= 0, rows, jnp.zeros_like(rows))
+        rows = x_ref[pl.ds(pl.multiple_of(jnp.maximum(source, 0) * BROWS, BROWS), BROWS), :]
+        placed_ref[s] = jnp.where(source >= 0, rows, jnp.zeros_like(rows))
         return carry
 
-    lax.fori_loop(0, slot_count, place, 0, unroll=8)
-
-
-def route(owner_list, candidates, collectors):
-    rows, width = candidates.shape
-    blocks = candidates.reshape(rows // BROWS, BROWS, width)
+    size = slot_count // parts
+    stores = []
+    for i in range(parts):
+        lax.fori_loop(i * size, (i + 1) * size, place, 0, unroll=8)
+        at = pl.ds(i * size, size)
+        store = pltpu.make_async_copy(placed_ref.at[at], out_hbm.at[at], out_sems.at[i])
+        store.start()
+        stores.append(store)
+    for copy in stores + copies[1:]:
+        copy.wait()
+
+
+def route(owners, kept, collectors):
+    candidates = kept[0]
+    _, width = candidates.shape
     slots = collectors * PAIR
+    parts = 4 if slots % 32 == 0 else 1
+    hbm = pl.BlockSpec(memory_space=pltpu.HBM)
+    vmem = pl.BlockSpec(memory_space=pltpu.VMEM)
     return pl.pallas_call(
         route_kernel,
-        out_shape=jax.ShapeDtypeStruct((slots, BROWS, width), candidates.dtype),
-        in_specs=[
-            pl.BlockSpec(memory_space=pltpu.SMEM),
-            pl.BlockSpec(memory_space=pltpu.VMEM),
+        out_shape=[jax.ShapeDtypeStruct((slots, BROWS, width), candidates.dtype)]
+        + [pltpu.VMEM(a.shape, a.dtype) for a in kept],
+        in_specs=[pl.BlockSpec(memory_space=pltpu.SMEM)] + [hbm] * len(kept),
+        out_specs=[hbm] + [vmem] * len(kept),
+        scratch_shapes=[
+            pltpu.VMEM((slots, BROWS, width), candidates.dtype),
+            pltpu.SMEM((slots,), jnp.int32),
+            pltpu.SemaphoreType.DMA((len(kept),)),
+            pltpu.SemaphoreType.DMA((parts,)),
         ],
-        out_specs=pl.BlockSpec(memory_space=pltpu.VMEM),
-        scratch_shapes=[pltpu.SMEM((slots,), jnp.int32)],
         name="route",
-    )(owner_list, blocks)
+    )(owners[:, 0], *kept)
 
 
 def score_kernel(
-    x_hbm, w1_hbm, b1_hbm, w2_hbm, b2_hbm, head_hbm, owners_hbm, out_ref,
-    x_ref, w1_ref, b1_ref, w2_ref, b2_ref, head_ref, owners_ref, hidden_ref, sums_ref, chooser_ref,
-    small_sem, w1_sem, w2_sem, *, tile_m, tile_h,
+    x_ref, w1_ref, b1_ref, b2_ref, head_ref, owners_ref, w2_hbm, out_ref,
+    w2_ref, hidden_ref, sums_ref, chooser_ref, w2_sem, *, tile_m, tile_h,
 ):
     rows = x_ref.shape[0]
     width = w1_ref.shape[1]
     slots, _, tile_n = w2_ref.shape
     tiles = w2_hbm.shape[1] // tile_n
-    first_tiles = w1_sem.shape[0]
-    columns = width // first_tiles
     blocks = rows // BROWS
     collectors = out_ref.shape[0]
-
-    pairs = (
-        (owners_hbm, owners_ref), (x_hbm, x_ref), (b1_hbm, b1_ref), (b2_hbm, b2_ref), (head_hbm, head_ref)
-    )
-    small = [pltpu.make_async_copy(a, b, small_sem.at[i]) for i, (a, b) in enumerate(pairs)]
-    firsts = [
-        pltpu.make_async_copy(
-            w1_hbm.at[:, pl.ds(i * columns, columns)], w1_ref.at[:, pl.ds(i * columns, columns)], w1_sem.at[i]
-        )
-        for i in range(first_tiles)
-    ]
 
     def load(j):
         at = pl.ds(pl.multiple_of(j * tile_n, tile_n), tile_n)
         return pltpu.make_async_copy(w2_hbm.at[:, at], w2_ref.at[j % slots], w2_sem.at[j % slots])
 
-    for copy in small[:3] + firsts + small[3:]:
-        copy.start()
+    load(0).start()
 
     sums_ref[...] = jnp.zeros_like(sums_ref)
-    small[0].wait()
+    for q in range(width // tile_h):
+        at = pl.ds(q * tile_h, tile_h)
+        first = jnp.dot(x_ref[...], w1_ref[:, at], preferred_element_type=jnp.float32)
+        first = first + b1_ref[:, at].astype(jnp.float32)
+        hidden_ref[:, at] = jnp.maximum(first, 0.0).astype(jnp.bfloat16)
+
     owner_row = jnp.broadcast_to(owners_ref[...], (blocks, blocks)).astype(jnp.float32)
     same_owner = owner_row == jnp.transpose(owner_row)
     before = lax.broadcasted_iota(jnp.int32, (blocks, blocks), 0) < lax.broadcasted_iota(
@@ -94,20 +116,6 @@
     for k in range(PAIR):
         slot = lax.broadcasted_iota(jnp.int32, (collectors, blocks), 0) * PAIR + k
         chooser_ref[k] = jnp.where(slot.astype(jnp.float32) == target, 1.0, 0.0).astype(jnp.bfloat16)
-
-    small[1].wait()
-    small[2].wait()
-    for i, copy in enumerate(firsts):
-        copy.wait()
-        if i == 0:
-            load(0).start()
-        for q in range(columns // tile_h):
-            at = pl.ds(i * columns + q * tile_h, tile_h)
-            first = jnp.dot(x_ref[...], w1_ref[:, at], preferred_element_type=jnp.float32)
-            first = first + b1_ref[:, at].astype(jnp.float32)
-            hidden_ref[:, at] = jnp.maximum(first, 0.0).astype(jnp.bfloat16)
-    small[3].wait()
-    small[4].wait()
 
     def second_layer(j, carry):
         load(j).wait()
@@ -136,30 +144,23 @@
         out_ref[:, k, :] = placed.astype(out_ref.dtype)
 
 
-def score(candidates, first_weight, first_bias, second_weight, second_bias, head_weight, owners, collectors):
+def score(kept, second_weight, collectors):
+    candidates, first_weight = kept[:2]
     rows, domains = candidates.shape
     width = first_weight.shape[1]
     outs = second_weight.shape[1]
-    blocks = owners.shape[0]
-    tile_n, tile_m, tile_h, first_tiles, slots = 512, 512, 512, 4, 2
+    blocks = rows // BROWS
+    tile_n, tile_m, tile_h, slots = 512, 512, 512, 2
     return pl.pallas_call(
         functools.partial(score_kernel, tile_m=tile_m, tile_h=tile_h),
         out_shape=jax.ShapeDtypeStruct((collectors, PAIR, BROWS), jnp.bfloat16),
-        in_specs=[pl.BlockSpec(memory_space=pltpu.HBM)] * 7,
+        in_specs=[pl.BlockSpec(memory_space=pltpu.VMEM)] * len(kept) + [pl.BlockSpec(memory_space=pltpu.HBM)],
         out_specs=pl.BlockSpec(memory_space=pltpu.VMEM),
         scratch_shapes=[
-            pltpu.VMEM((rows, domains), candidates.dtype),
-            pltpu.VMEM((domains, width), first_weight.dtype),
-            pltpu.VMEM((1, width), first_bias.dtype),
             pltpu.VMEM((slots, width, tile_n), second_weight.dtype),
-            pltpu.VMEM((1, outs), second_bias.dtype),
-            pltpu.VMEM((1, outs), head_weight.dtype),
-            pltpu.VMEM((1, blocks), owners.dtype),
             pltpu.VMEM((rows, width), jnp.bfloat16),
             pltpu.VMEM((rows, LANES), jnp.float32),
             pltpu.VMEM((PAIR, collectors, blocks), jnp.bfloat16),
-            pltpu.SemaphoreType.DMA((5,)),
-            pltpu.SemaphoreType.DMA((first_tiles,)),
             pltpu.SemaphoreType.DMA((slots,)),
         ],
         compiler_params=pltpu.CompilerParams(vmem_limit_bytes=VMEM_GRANT),
@@ -169,32 +170,36 @@
             bytes_accessed=2 * (rows * domains + domains * width + width * outs),
         ),
         name="score",
-    )(
-        candidates, first_weight, first_bias, second_weight, second_bias.reshape(1, -1),
-        head_weight.reshape(1, -1), owners.reshape(1, -1),
-    )
-
-
-def settle_kernel(arrived_hbm, out_hbm, sems):
-    parts = sems.shape[0]
+    )(*kept, second_weight)
+
+
+def settle_kernel(arrived_hbm, out_hbm, buffer_ref, in_sems, out_sems):
+    parts = in_sems.shape[0]
     size = arrived_hbm.shape[0] // parts
-    copies = [
-        pltpu.make_async_copy(arrived_hbm.at[pl.ds(i * size, size)], out_hbm.at[pl.ds(i * size, size)], sems.at[i])
-        for i in range(parts)
-    ]
-    for copy in copies:
-        copy.start()
-    for copy in copies:
-        copy.wait()
+    slices = [pl.ds(i * size, size) for i in range(parts)]
+    fetches = [pltpu.make_async_copy(arrived_hbm.at[at], buffer_ref.at[at], in_sems.at[i]) for i, at in enumerate(slices)]
+    stores = [pltpu.make_async_copy(buffer_ref.at[at], out_hbm.at[at], out_sems.at[i]) for i, at in enumerate(slices)]
+    for fetch in fetches:
+        fetch.start()
+    for fetch, store in zip(fetches, stores):
+        fetch.wait()
+        store.start()
+    for store in stores:
+        store.wait()
 
 
 def settle(arrived):
+    parts = 4 if arrived.shape[0] % 4 == 0 else 1
     return pl.pallas_call(
         settle_kernel,
         out_shape=jax.ShapeDtypeStruct(arrived.shape, arrived.dtype),
         in_specs=[pl.BlockSpec(memory_space=pltpu.HBM)],
         out_specs=pl.BlockSpec(memory_space=pltpu.HBM),
-        scratch_shapes=[pltpu.SemaphoreType.DMA((8 if arrived.shape[0] % 8 == 0 else 1,))],
+        scratch_shapes=[
+            pltpu.VMEM(arrived.shape, arrived.dtype),
+            pltpu.SemaphoreType.DMA((parts,)),
+            pltpu.SemaphoreType.DMA((parts,)),
+        ],
         name="settle",
     )(arrived)
 
@@ -206,13 +211,14 @@
         )
     collectors = lax.axis_size("dp")
     width = candidates.shape[1]
-    outgoing = route(owners[:, 0], candidates, collectors)
+    kept = (
+        candidates, first_weight, first_bias, second_bias.reshape(1, -1), head_weight.reshape(1, -1),
+        owners.reshape(1, -1),
+    )
+    outgoing, *kept = route(owners, kept, collectors)
     outgoing = outgoing.reshape(collectors, PAIR, BROWS, width)
     arrived = lax.all_to_all(outgoing, "dp", split_axis=0, concat_axis=0, tiled=True)
-    outgoing_scores = score(
-        candidates, first_weight, first_bias, second_weight, second_bias, head_weight, owners,
-        collectors,
-    )
+    outgoing_scores = score(kept, second_weight, collectors)
     arrived, outgoing_scores = lax.optimization_barrier((arrived, outgoing_scores))
     arrived_scores = lax.all_to_all(outgoing_scores, "dp", split_axis=0, concat_axis=0, tiled=True)
     collected = settle(arrived.reshape(collectors * PAIR, BROWS, width))

time: 91.5 us -> 66.9 us (0.73)
  Pallas kernels: 76.6 us -> 46.8 us
  waiting for transfers between devices: 0.01 us -> 5.19 us
    pallas_call x1, Pallas kernels: 32.9 us -> 1.98 us  [settle(): pl.pallas_call(settle_kernel, out_shape=jax.ShapeDtypeStruct(arrived.shap...]
    all_to_all x1, waiting for transfers between devices: 0.01 us -> 5.19 us  [local(): lax.all_to_all(outgoing_scores, 'dp', split_axis=0, concat_axis=0, tiled=...]
  transfers between devices with their start and end apart: 2 -> 2, of which waited for: 0 -> 1; matrix products, arithmetic and copies ran while one was open for 0% -> 0% of each run, Pallas kernels for 81% -> 66%
where the time goes in v3:
time: 66.9 us; the launch traced here: 66.5 us
  Pallas kernels  46.8 us (70%)
  starting transfers between devices  13.2 us (20%)
  waiting for transfers between devices  5.19 us (8%)
  local copies, waits for them, and re-layouts  0.68 us (1%)
  between operations  0.68 us (1%)
    pallas_call x1, Pallas kernels, score(): pl.pallas_call(functools.partial(score_kernel, tile_m=tile_m, tile_h=tile...  42 us
    all_to_all x1, starting transfers between devices, local(): lax.all_to_all(outgoing, 'dp', split_axis=0, concat_axis=0, tiled=True)  7.46 us
    all_to_all x1, starting transfers between devices, local(): lax.all_to_all(outgoing_scores, 'dp', split_axis=0, concat_axis=0, tiled=...  5.77 us
    all_to_all x1, waiting for transfers between devices, local(): lax.all_to_all(outgoing_scores, 'dp', split_axis=0, concat_axis=0, tiled=...  5.19 us
    pallas_call x1, Pallas kernels, route(): pl.pallas_call(route_kernel, out_shape=[jax.ShapeDtypeStruct((slots, BROW...  2.8 us
    pallas_call x1, Pallas kernels, settle(): pl.pallas_call(settle_kernel, out_shape=jax.ShapeDtypeStruct(arrived.shap...  1.98 us
  transfers between devices with their start and end apart: 2, of which 1 were waited for; matrix products, arithmetic and copies ran while one was open for 0% of the time, Pallas kernels for 66%

profile of v3, /device:TPU:0, one launch (start us, length us, event | category | flops | bytes accessed | tf_op | source)
XLA Modules:
  0.0 66.5 jit_solution(16134481272997590808)
XLA Ops:
  0.6 2.8 %route.1 = (bf16[64,32,256]{2,1,0:T(8,128)(2,1)}, bf16[1024,256]{1,0:T(8,128)(2,1)S(1)}, bf16[256,4096]{1,0:T(8,128)(2,1)S(1)}, bf16[1,4096]{1,0:T(2,128)(2,1)S(...) custom-call(s32[32]{0:T(128)} %bitcast.11, bf16[1024,256]{1,0:T(8,128)(2,1)} %x_hbm.1, ...), custom_call_target="tpu_custom_call" | custom-call | tf_op jit(solution)/shard_map/route/pallas_call | solution.py:69
  3.4 7.5 %all-to-all-start = ((bf16[32,2,32,256]{3,2,1,0:T(8,128)(2,1)}), bf16[32,2,32,256]{3,2,1,0:T(8,128)(2,1)}, u32[]{:S(2)}, u32[]{:S(2)}) async-start(bf16[32,2,32,256]{3,2,1,0:T(8,128)(2,1)} %bitcast.7), calls=%async_computation | async-start | bytes 2097152 | tf_op jit(solution)/shard_map/all_to_all | solution.py:220
  10.9 42.0 %score.1 = bf16[32,2,32]{2,1,0:T(2,128)(2,1)} custom-call(bf16[1024,256]{1,0:T(8,128)(2,1)S(1)} %get-tuple-element.12.x_ref, bf16[256,4096]{1,0:T(8,128)(2,1)S(1)} %get-tuple-element.13.w1_ref, bf16[1,4096]{1,0:T(2,128)(2,1)S(1)} %get-tuple-element.14.b1_ref, f32[1,4096]{1,0:T(1,128)S(1)} %get-tuple-element.15.b2_ref, ...), custom_call_target="tpu_custom_call" | custom-call | flops 36507222016 | bytes 36175872 | tf_op jit(solution)/shard_map/score/pallas_call | solution.py:154
  52.9 0.0 all-to-all-done
  52.9 5.8 %all-to-all-start.1 = ((bf16[32,2,32]{2,1,0:T(2,128)(2,1)}), bf16[32,2,32]{2,1,0:T(2,128)(2,1)S(1)}, u32[]{:S(2)}, u32[]{:S(2)}) async-start(bf16[32,2,32]{2,1,0:T(2,128)(2,1)} %score.1), calls=%async_computation.1 | async-start | bytes 32768 | tf_op jit(solution)/shard_map/all_to_all | solution.py:223
  58.7 2.0 %settle.1 = bf16[64,32,256]{2,1,0:T(8,128)(2,1)} custom-call(bf16[64,32,256]{2,1,0:T(8,128)(2,1)} %bitcast.5.arrived_hbm), custom_call_target="tpu_custom_call" | custom-call | tf_op jit(solution)/shard_map/settle/pallas_call | solution.py:193
  60.7 5.2 %all-to-all-done.1 = bf16[32,2,32]{2,1,0:T(2,128)(2,1)S(1)} async-done(((bf16[32,2,32]{2,1,0:T(2,128)(2,1)}), bf16[32,2,32]{2,1,0:T(2,128)(2,1)S(1)}, u32[]{:S(2)}, u32[]{:S(2)}) %all-to-all-start.1) | async-done | bytes 4128 | tf_op jit(solution)/shard_map/all_to_all | solution.py:223
  65.9 0.7 %copy.9 = bf16[64,32]{0,1:T(8,128)(2,1)} copy(bf16[64,32]{1,0:T(8,128)(2,1)S(1)} %bitcast.8) | data formatting | bytes 8192
Async XLA Ops:
  3.4 49.5 %all-to-all-start = ((bf16[32,2,32,256]{3,2,1,0:T(8,128)(2,1)}), bf16[32,2,32,256]{3,2,1,0:T(8,128)(2,1)}, u32[]{:S(2)}, u32[]{:S(2)}) async-start(bf16[32,2,32,256]{3,2,1,0:T(8,128)(2,1)} %bitcast.7), calls=%async_computation | async-start | bytes 2097152 | tf_op jit(solution)/shard_map/all_to_all | solution.py:220
  52.9 12.9 %all-to-all-start.1 = ((bf16[32,2,32]{2,1,0:T(2,128)(2,1)}), bf16[32,2,32]{2,1,0:T(2,128)(2,1)S(1)}, u32[]{:S(2)}, u32[]{:S(2)}) async-start(bf16[32,2,32]{2,1,0:T(2,128)(2,1)} %score.1), calls=%async_computation.1 | async-start | bytes 32768 | tf_op jit(solution)/shard_map/all_to_all | solution.py:223

commit v4 on v3

--- a/solution.py
+++ b/solution.py
@@ -12,6 +12,7 @@
 PAIR = 2
 LANES = 128
 VMEM_GRANT = 36 << 20
+FIRST_STEPS = 2
 
 
 def route_kernel(
@@ -100,11 +101,17 @@
     load(0).start()
 
     sums_ref[...] = jnp.zeros_like(sums_ref)
-    for q in range(width // tile_h):
-        at = pl.ds(q * tile_h, tile_h)
-        first = jnp.dot(x_ref[...], w1_ref[:, at], preferred_element_type=jnp.float32)
-        first = first + b1_ref[:, at].astype(jnp.float32)
-        hidden_ref[:, at] = jnp.maximum(first, 0.0).astype(jnp.bfloat16)
+
+    def first_layer(i, carry):
+        for q in range(width // tile_h // FIRST_STEPS):
+            start = pl.multiple_of(i * (width // FIRST_STEPS) + q * tile_h, tile_h)
+            at = pl.ds(start, tile_h)
+            first = jnp.dot(x_ref[...], w1_ref[:, at], preferred_element_type=jnp.float32)
+            first = first + b1_ref[:, at].astype(jnp.float32)
+            hidden_ref[:, at] = jnp.maximum(first, 0.0).astype(jnp.bfloat16)
+        return carry
+
+    lax.fori_loop(0, FIRST_STEPS, first_layer, 0)
 
     owner_row = jnp.broadcast_to(owners_ref[...], (blocks, blocks)).astype(jnp.float32)
     same_owner = owner_row == jnp.transpose(owner_row)

time: 66.9 us -> 65.1 us (0.973)
  Pallas kernels: 46.8 us -> 45 us
    pallas_call x1, Pallas kernels: 42 us -> 40.2 us  [score(): pl.pallas_call(functools.partial(score_kernel, tile_m=tile_m, tile_h=tile...]
  transfers between devices with their start and end apart: 2 -> 2, of which waited for: 1 -> 1; matrix products, arithmetic and copies ran while one was open for 0% -> 0% of each run, Pallas kernels for 66% -> 65%
where the time goes in v4:
time: 65.1 us; the launch traced here: 64.8 us
  Pallas kernels  45 us (69%)
  starting transfers between devices  13.2 us (20%)
  waiting for transfers between devices  5.19 us (8%)
  local copies, waits for them, and re-layouts  0.68 us (1%)
  between operations  0.68 us (1%)
    pallas_call x1, Pallas kernels, score(): pl.pallas_call(functools.partial(score_kernel, tile_m=tile_m, tile_h=tile...  40.2 us
    all_to_all x1, starting transfers between devices, local(): lax.all_to_all(outgoing, 'dp', split_axis=0, concat_axis=0, tiled=True)  7.46 us
    all_to_all x1, starting transfers between devices, local(): lax.all_to_all(outgoing_scores, 'dp', split_axis=0, concat_axis=0, tiled=...  5.76 us
    all_to_all x1, waiting for transfers between devices, local(): lax.all_to_all(outgoing_scores, 'dp', split_axis=0, concat_axis=0, tiled=...  5.19 us
    pallas_call x1, Pallas kernels, route(): pl.pallas_call(route_kernel, out_shape=[jax.ShapeDtypeStruct((slots, BROW...  2.8 us
    pallas_call x1, Pallas kernels, settle(): pl.pallas_call(settle_kernel, out_shape=jax.ShapeDtypeStruct(arrived.shap...  1.98 us
  transfers between devices with their start and end apart: 2, of which 1 were waited for; matrix products, arithmetic and copies ran while one was open for 0% of the time, Pallas kernels for 65%

profile of v4, /device:TPU:0, one launch (start us, length us, event | category | flops | bytes accessed | tf_op | source)
XLA Modules:
  0.0 64.8 jit_solution(8074379867799404324)
XLA Ops:
  0.6 2.8 %route.1 = (bf16[64,32,256]{2,1,0:T(8,128)(2,1)}, bf16[1024,256]{1,0:T(8,128)(2,1)S(1)}, bf16[256,4096]{1,0:T(8,128)(2,1)S(1)}, bf16[1,4096]{1,0:T(2,128)(2,1)S(...) custom-call(s32[32]{0:T(128)} %bitcast.11, bf16[1024,256]{1,0:T(8,128)(2,1)} %x_hbm.1, ...), custom_call_target="tpu_custom_call" | custom-call | tf_op jit(solution)/shard_map/route/pallas_call | solution.py:70
  3.4 7.5 %all-to-all-start = ((bf16[32,2,32,256]{3,2,1,0:T(8,128)(2,1)}), bf16[32,2,32,256]{3,2,1,0:T(8,128)(2,1)}, u32[]{:S(2)}, u32[]{:S(2)}) async-start(bf16[32,2,32,256]{3,2,1,0:T(8,128)(2,1)} %bitcast.7), calls=%async_computation | async-start | bytes 2097152 | tf_op jit(solution)/shard_map/all_to_all | solution.py:227
  10.9 40.2 %score.1 = bf16[32,2,32]{2,1,0:T(2,128)(2,1)} custom-call(bf16[1024,256]{1,0:T(8,128)(2,1)S(1)} %get-tuple-element.12.x_ref, bf16[256,4096]{1,0:T(8,128)(2,1)S(1)} %get-tuple-element.13.w1_ref, bf16[1,4096]{1,0:T(2,128)(2,1)S(1)} %get-tuple-element.14.b1_ref, f32[1,4096]{1,0:T(1,128)S(1)} %get-tuple-element.15.b2_ref, ...), custom_call_target="tpu_custom_call" | custom-call | flops 36507222016 | bytes 36175872 | tf_op jit(solution)/shard_map/score/pallas_call | solution.py:161
  51.1 0.0 all-to-all-done
  51.2 5.8 %all-to-all-start.1 = ((bf16[32,2,32]{2,1,0:T(2,128)(2,1)}), bf16[32,2,32]{2,1,0:T(2,128)(2,1)S(1)}, u32[]{:S(2)}, u32[]{:S(2)}) async-start(bf16[32,2,32]{2,1,0:T(2,128)(2,1)} %score.1), calls=%async_computation.1 | async-start | bytes 32768 | tf_op jit(solution)/shard_map/all_to_all | solution.py:230
  56.9 2.0 %settle.1 = bf16[64,32,256]{2,1,0:T(8,128)(2,1)} custom-call(bf16[64,32,256]{2,1,0:T(8,128)(2,1)} %bitcast.5.arrived_hbm), custom_call_target="tpu_custom_call" | custom-call | tf_op jit(solution)/shard_map/settle/pallas_call | solution.py:200
  58.9 5.2 %all-to-all-done.1 = bf16[32,2,32]{2,1,0:T(2,128)(2,1)S(1)} async-done(((bf16[32,2,32]{2,1,0:T(2,128)(2,1)}), bf16[32,2,32]{2,1,0:T(2,128)(2,1)S(1)}, u32[]{:S(2)}, u32[]{:S(2)}) %all-to-all-start.1) | async-done | bytes 4128 | tf_op jit(solution)/shard_map/all_to_all | solution.py:230
  64.1 0.7 %copy.9 = bf16[64,32]{0,1:T(8,128)(2,1)} copy(bf16[64,32]{1,0:T(8,128)(2,1)S(1)} %bitcast.8) | data formatting | bytes 8192
Async XLA Ops:
  3.4 47.7 %all-to-all-start = ((bf16[32,2,32,256]{3,2,1,0:T(8,128)(2,1)}), bf16[32,2,32,256]{3,2,1,0:T(8,128)(2,1)}, u32[]{:S(2)}, u32[]{:S(2)}) async-start(bf16[32,2,32,256]{3,2,1,0:T(8,128)(2,1)} %bitcast.7), calls=%async_computation | async-start | bytes 2097152 | tf_op jit(solution)/shard_map/all_to_all | solution.py:227
  51.2 12.9 %all-to-all-start.1 = ((bf16[32,2,32]{2,1,0:T(2,128)(2,1)}), bf16[32,2,32]{2,1,0:T(2,128)(2,1)S(1)}, u32[]{:S(2)}, u32[]{:S(2)}) async-start(bf16[32,2,32]{2,1,0:T(2,128)(2,1)} %score.1), calls=%async_computation.1 | async-start | bytes 32768 | tf_op jit(solution)/shard_map/all_to_all | solution.py:230
